TPU v7x, 32 devices: a whole 2x2x4 slice. The times are simulated.
32 devices in a mesh: dp: 8 (over y, x, core), fsdp: 4 (over z).
Axes of the slice: x: 2, y: 2, z: 4, core: 2. Of those that a mesh axis runs over, the one named last changes fastest.
Arguments:
- tokens: bfloat16 [32768, 768], P(('dp', 'fsdp')), may hold values from -8 to 8
- chip_ids: int32 [32768], P(('dp', 'fsdp')), may hold values from 0 to 511, as said below
- ln1_gain: bfloat16 [768], P('fsdp'), may hold values from 0.5 to 1.5
- ln1_bias: bfloat16 [768], P('fsdp'), may hold values from -1.5 to 1.5
- w_qkv: bfloat16 [768, 2304], P('fsdp'), may hold values from -0.3125 to 0.3125
- w_out: bfloat16 [768, 768], P('fsdp'), may hold values from -0.625 to 0.625
- b_out: bfloat16 [768], P('fsdp'), may hold values from -1.5 to 1.5
- ln2_gain: bfloat16 [768], P('fsdp'), may hold values from 0.5 to 1.5
- ln2_bias: bfloat16 [768], P('fsdp'), may hold values from -1.5 to 1.5
- w_fc1: bfloat16 [768, 3072], P('fsdp'), may hold values from -0.21875 to 0.21875
- b_fc1: bfloat16 [3072], P('fsdp'), may hold values from -2.5 to 2.5
- w_fc2: bfloat16 [3072, 768], P('fsdp'), may hold values from -0.15625 to 0.15625
- b_fc2: bfloat16 [768], P('fsdp'), may hold values from -1.5 to 1.5
- cotangent: bfloat16 [32768, 768], P(('dp', 'fsdp')), may hold values from -6 to 6
Outputs:
- layer_out: bfloat16 [32768, 768], P(('dp', 'fsdp'))
- grad_tokens: float32 [32768, 768], P(('dp', 'fsdp'))
- grad_ln1_gain: float32 [768], P('fsdp')
- grad_ln1_bias: float32 [768], P('fsdp')
- grad_w_qkv: float32 [768, 2304], P('fsdp')
- grad_w_out: float32 [768, 768], P('fsdp')
- grad_b_out: float32 [768], P('fsdp')
- grad_ln2_gain: float32 [768], P('fsdp')
- grad_ln2_bias: float32 [768], P('fsdp')
- grad_w_fc1: float32 [768, 3072], P('fsdp')
- grad_b_fc1: float32 [3072], P('fsdp')
- grad_w_fc2: float32 [3072, 768], P('fsdp')
- grad_b_fc2: float32 [768], P('fsdp')
Inputs may be any that keep to these rules, and one draw needn't show every extreme that they name: `chip_ids`: chip numbers never fall along the tokens. Each chip holds exactly 64 or 256 tokens and lies inside one device's block of 1024 rows; every such block holds at least one chip of 256 tokens and may hold only such chips. The chips of the d-th block of rows carry numbers from d * 16 to (d + 1) * 16 - 1, the first and the last of them always used.
All inputs are finite; a program needn't handle non-finite values.
Results may differ from a plain program's by a relative error of at most 0.015.
Values may be sent and summed in bfloat16 or wider, within the bound.
No kernel may reach another device: no remote copies, remote signals or barrier semaphores. Data moves between devices by JAX's collectives and lax.ppermute only.
A program may use at most 320 MiB of HBM per device.

v0:
```python
import math
import jax
import jax.numpy as jnp
from jax import lax
from jax.sharding import PartitionSpec as P

HEADS = 12
epsilon = 1e-05
neg_big = -1e30
inv_sqrt_two = 1.0 / math.sqrt(2.0)
inv_sqrt_tau = 1.0 / math.sqrt(2.0 * math.pi)


def layer_norm(token_rows, gain_vec, shift_vec):
    centred = token_rows - jnp.mean(token_rows, axis=-1, keepdims=True)
    inverse = lax.rsqrt(jnp.mean(centred * centred, axis=-1, keepdims=True) + epsilon)
    normed = centred * inverse
    return (normed * gain_vec + shift_vec, normed, inverse)


def norm_back(grad_rows, normed, inverse, gain_vec):
    d_gain = jnp.sum(grad_rows * normed, axis=0)
    d_shift = jnp.sum(grad_rows, axis=0)
    inner_grad = grad_rows * gain_vec
    d_rows = inverse * (
        inner_grad
        - jnp.mean(inner_grad, axis=-1, keepdims=True)
        - normed * jnp.mean(inner_grad * normed, axis=-1, keepdims=True)
    )
    return (d_rows, d_gain, d_shift)


def weight_grad(left_side, right_side):
    return lax.dot_general(
        left_side, right_side, (((0,), (0,)), ((), ())), preferred_element_type=jnp.float32
    )


def input_grad(grad_side, weight):
    return lax.dot_general(
        grad_side, weight, (((1,), (1,)), ((), ())), preferred_element_type=jnp.float32
    )


def head_major(qkv_all):
    length = qkv_all.shape[0]
    head_size = qkv_all.shape[1] // (3 * HEADS)
    stacked = qkv_all.reshape(length, 3, HEADS, head_size).transpose(1, 2, 0, 3)
    return (stacked[0], stacked[1], stacked[2], 1.0 / math.sqrt(head_size))


def block_scores(query_block, key_heads, chip_block, chip_ids, scale_factor):
    scores = (
        jnp.einsum("hqe,hke->hqk", query_block, key_heads, preferred_element_type=jnp.float32)
        * scale_factor
    )
    same_chip = chip_block[:, None] == chip_ids[None, :]
    return jnp.where(same_chip[None], scores, neg_big)


def attend(qkv_all, chip_ids):
    queries, key_heads, value_heads, scale_factor = head_major(qkv_all)
    length = qkv_all.shape[0]
    block = min(512, length)
    mixed_parts = []
    sum_parts = []
    for start in range(0, length, block):
        scores = block_scores(
            queries[:, start : start + block],
            key_heads,
            chip_ids[start : start + block],
            chip_ids,
            scale_factor,
        )
        row_max = jnp.max(scores, axis=-1, keepdims=True)
        exp_score = jnp.exp(scores - row_max)
        row_total = jnp.sum(exp_score, axis=-1, keepdims=True)
        probs_low = (exp_score / row_total).astype(jnp.bfloat16)
        mixed_parts.append(
            jnp.einsum("hqk,hke->hqe", probs_low, value_heads, preferred_element_type=jnp.float32)
        )
        sum_parts.append(row_max + jnp.log(row_total))
    mixed = jnp.concatenate(mixed_parts, axis=1)
    return (mixed.transpose(1, 0, 2).reshape(length, -1), sum_parts)


def attend_back(qkv_all, chip_ids, sum_parts, grad_low):
    queries, key_heads, value_heads, scale_factor = head_major(qkv_all)
    length = qkv_all.shape[0]
    head_size = queries.shape[2]
    grad_heads = grad_low.reshape(length, HEADS, head_size).transpose(1, 0, 2)
    block = min(512, length)
    d_keys = jnp.zeros(key_heads.shape, jnp.float32)
    d_values = jnp.zeros(value_heads.shape, jnp.float32)
    query_parts = []
    for number, start in enumerate(range(0, length, block)):
        query_block = queries[:, start : start + block]
        grad_block = grad_heads[:, start : start + block]
        scores = block_scores(
            query_block, key_heads, chip_ids[start : start + block], chip_ids, scale_factor
        )
        attn_probs = jnp.exp(scores - sum_parts[number])
        probs_low = attn_probs.astype(jnp.bfloat16)
        d_values = d_values + jnp.einsum(
            "hqk,hqe->hke", probs_low, grad_block, preferred_element_type=jnp.float32
        )
        d_probs = jnp.einsum(
            "hqe,hke->hqk", grad_block, value_heads, preferred_element_type=jnp.float32
        )
        d_score = (
            attn_probs * (d_probs - jnp.sum(d_probs * attn_probs, axis=-1, keepdims=True))
        ).astype(jnp.bfloat16)
        query_parts.append(
            jnp.einsum("hqk,hke->hqe", d_score, key_heads, preferred_element_type=jnp.float32)
            * scale_factor
        )
        d_keys = (
            d_keys
            + jnp.einsum("hqk,hqe->hke", d_score, query_block, preferred_element_type=jnp.float32)
            * scale_factor
        )
    d_query = jnp.concatenate(query_parts, axis=1)
    combined = (
        jnp.stack([d_query, d_keys, d_values], axis=0).transpose(2, 0, 1, 3).reshape(length, -1)
    )
    return combined.astype(jnp.bfloat16)


def on_device(
    tokens,
    chip_ids,
    ln1_gain,
    ln1_bias,
    w_qkv,
    w_out,
    b_out,
    ln2_gain,
    ln2_bias,
    w_fc1,
    b_fc1,
    w_fc2,
    b_fc2,
    cotangent,
):
    gathered = (
        lax.all_gather(ln1_gain, "fsdp", axis=0, tiled=True),
        lax.all_gather(ln1_bias, "fsdp", axis=0, tiled=True),
        lax.all_gather(w_qkv, "fsdp", axis=0, tiled=True),
        lax.all_gather(w_out, "fsdp", axis=0, tiled=True),
        lax.all_gather(b_out, "fsdp", axis=0, tiled=True),
        lax.all_gather(ln2_gain, "fsdp", axis=0, tiled=True),
        lax.all_gather(ln2_bias, "fsdp", axis=0, tiled=True),
        lax.all_gather(w_fc1, "fsdp", axis=0, tiled=True),
        lax.all_gather(b_fc1, "fsdp", axis=0, tiled=True),
        lax.all_gather(w_fc2, "fsdp", axis=0, tiled=True),
        lax.all_gather(b_fc2, "fsdp", axis=0, tiled=True),
    )
    gain_one = gathered[0].astype(jnp.float32)
    gain_two = gathered[5].astype(jnp.float32)
    as_float = tokens.astype(jnp.float32)
    normed_in_f, normed_one, inverse_one = layer_norm(
        as_float, gain_one, gathered[1].astype(jnp.float32)
    )
    normed_in = normed_in_f.astype(jnp.bfloat16)
    qkv_all = jnp.dot(normed_in, gathered[2], preferred_element_type=jnp.float32).astype(
        jnp.bfloat16
    )
    attn_mixed, sum_parts = attend(qkv_all, chip_ids)
    mixed_low = attn_mixed.astype(jnp.bfloat16)
    hidden_one = as_float + (
        jnp.dot(mixed_low, gathered[3], preferred_element_type=jnp.float32)
        + gathered[4].astype(jnp.float32)
    )
    normed_mid_f, normed_two, inverse_two = layer_norm(
        hidden_one, gain_two, gathered[6].astype(jnp.float32)
    )
    normed_mid = normed_mid_f.astype(jnp.bfloat16)
    pre_act = jnp.dot(normed_mid, gathered[7], preferred_element_type=jnp.float32) + gathered[
        8
    ].astype(jnp.float32)
    activated = jax.nn.gelu(pre_act, approximate=False).astype(jnp.bfloat16)
    output = hidden_one + (
        jnp.dot(activated, gathered[9], preferred_element_type=jnp.float32)
        + gathered[10].astype(jnp.float32)
    )
    gathered = (
        lax.all_gather(ln1_gain, "fsdp", axis=0, tiled=True),
        lax.all_gather(ln1_bias, "fsdp", axis=0, tiled=True),
        lax.all_gather(w_qkv, "fsdp", axis=0, tiled=True),
        lax.all_gather(w_out, "fsdp", axis=0, tiled=True),
        lax.all_gather(b_out, "fsdp", axis=0, tiled=True),
        lax.all_gather(ln2_gain, "fsdp", axis=0, tiled=True),
        lax.all_gather(ln2_bias, "fsdp", axis=0, tiled=True),
        lax.all_gather(w_fc1, "fsdp", axis=0, tiled=True),
        lax.all_gather(b_fc1, "fsdp", axis=0, tiled=True),
        lax.all_gather(w_fc2, "fsdp", axis=0, tiled=True),
        lax.all_gather(b_fc2, "fsdp", axis=0, tiled=True),
    )
    grad_out = cotangent.astype(jnp.float32)
    d_b_fc2 = jnp.sum(cotangent.astype(jnp.float32), axis=0)
    d_w_fc2 = weight_grad(activated, cotangent)
    d_act = input_grad(cotangent, gathered[9])
    slope = (
        0.5 * (1.0 + jax.scipy.special.erf(pre_act * inv_sqrt_two))
        + pre_act * jnp.exp(-0.5 * pre_act * pre_act) * inv_sqrt_tau
    )
    d_pre_low = (d_act * slope).astype(jnp.bfloat16)
    d_b_fc1 = jnp.sum(d_pre_low.astype(jnp.float32), axis=0)
    d_w_fc1 = weight_grad(normed_mid, d_pre_low)
    d_mid = input_grad(d_pre_low, gathered[7])
    d_hidden_norm, d_ln2_gain, d_ln2_bias = norm_back(d_mid, normed_two, inverse_two, gain_two)
    d_hidden = grad_out + d_hidden_norm
    d_hidden_low = d_hidden.astype(jnp.bfloat16)
    d_b_out = jnp.sum(d_hidden_low.astype(jnp.float32), axis=0)
    d_w_out = weight_grad(mixed_low, d_hidden_low)
    d_mixed = input_grad(d_hidden_low, gathered[3]).astype(jnp.bfloat16)
    d_qkv = attend_back(qkv_all, chip_ids, sum_parts, d_mixed)
    d_w_qkv = weight_grad(normed_in, d_qkv)
    d_in = input_grad(d_qkv, gathered[2])
    d_in_norm, d_ln1_gain, d_ln1_bias = norm_back(d_in, normed_one, inverse_one, gain_one)
    d_tokens = d_hidden + d_in_norm
    all_rows = (
        lax.psum_scatter(
            d_ln1_gain.astype(jnp.bfloat16), "fsdp", scatter_dimension=0, tiled=True
        ).astype(jnp.float32),
        lax.psum_scatter(
            d_ln1_bias.astype(jnp.bfloat16), "fsdp", scatter_dimension=0, tiled=True
        ).astype(jnp.float32),
        lax.psum_scatter(
            d_w_qkv.astype(jnp.bfloat16), "fsdp", scatter_dimension=0, tiled=True
        ).astype(jnp.float32),
        lax.psum_scatter(
            d_w_out.astype(jnp.bfloat16), "fsdp", scatter_dimension=0, tiled=True
        ).astype(jnp.float32),
        lax.psum_scatter(
            d_b_out.astype(jnp.bfloat16), "fsdp", scatter_dimension=0, tiled=True
        ).astype(jnp.float32),
        lax.psum_scatter(
            d_ln2_gain.astype(jnp.bfloat16), "fsdp", scatter_dimension=0, tiled=True
        ).astype(jnp.float32),
        lax.psum_scatter(
            d_ln2_bias.astype(jnp.bfloat16), "fsdp", scatter_dimension=0, tiled=True
        ).astype(jnp.float32),
        lax.psum_scatter(
            d_w_fc1.astype(jnp.bfloat16), "fsdp", scatter_dimension=0, tiled=True
        ).astype(jnp.float32),
        lax.psum_scatter(
            d_b_fc1.astype(jnp.bfloat16), "fsdp", scatter_dimension=0, tiled=True
        ).astype(jnp.float32),
        lax.psum_scatter(
            d_w_fc2.astype(jnp.bfloat16), "fsdp", scatter_dimension=0, tiled=True
        ).astype(jnp.float32),
        lax.psum_scatter(
            d_b_fc2.astype(jnp.bfloat16), "fsdp", scatter_dimension=0, tiled=True
        ).astype(jnp.float32),
    )
    final_grads = tuple(
        lax.psum(
            (
                all_rows[0],
                all_rows[1],
                all_rows[2],
                all_rows[3],
                all_rows[4],
                all_rows[5],
                all_rows[6],
                all_rows[7],
                all_rows[8],
                all_rows[9],
                all_rows[10],
            ),
            "dp",
        )
    )
    return (output.astype(jnp.bfloat16), d_tokens) + final_grads


def solution(mesh):
    placed = (
        P(("dp", "fsdp"), None),
        P(("dp", "fsdp")),
        P("fsdp"),
        P("fsdp"),
        P("fsdp", None),
        P("fsdp", None),
        P("fsdp"),
        P("fsdp"),
        P("fsdp"),
        P("fsdp", None),
        P("fsdp"),
        P("fsdp", None),
        P("fsdp"),
        P(("dp", "fsdp"), None),
    )
    return jax.shard_map(
        on_device,
        mesh=mesh,
        in_specs=placed,
        out_specs=(
            P(("dp", "fsdp"), None),
            P(("dp", "fsdp"), None),
            P("fsdp"),
            P("fsdp"),
            P("fsdp", None),
            P("fsdp", None),
            P("fsdp"),
            P("fsdp"),
            P("fsdp"),
            P("fsdp", None),
            P("fsdp"),
            P("fsdp", None),
            P("fsdp"),
        ),
        check_vma=False,
    )
```

profile of v0, /device:TPU:0, one launch (start us, length us, event | category | flops | bytes accessed | tf_op | source)
XLA Modules:
  0.0 876.6 jit_solution(12832730221961627232)
XLA Ops:
  16.2 21.8 %all-reduce.15 = (bf16[768]{0:T(1024)(128)(2,1)S(1)}, bf16[768]{0:T(1024)(128)(2,1)S(1)}, bf16[768]{0:T(1024)(128)(2,1)S(1)}, bf16[768]{0:T(1024)(128)(2,1)S(1)}, bf16[768]{0:T(1024)(128)(2,1)S(1)}) all-reduce(bf16[768]{0:T(1024)(128)(2,1)S(1)} %dynamic-update-slice.1, ...), channel_id=1, replica_groups=mesh['dp'=8,'fsdp'=4] {'fsdp'}, use_global_device_ids=true, to_apply=%add.1 | all-reduce | flops 3840 | bytes 15360
  41.8 14.0 %all-gather = bf16[4,1,768]{2,1,0:T(2,128)(2,1)S(1)} all-gather(bf16[1,1,768]{2,1,0:T(2,128)(2,1)S(1)} %reshape.178), channel_id=1, replica_groups=mesh['dp'=8,'fsdp'=4] {'fsdp'}, dimensions={0}, use_global_device_ids=true | all-gather | bytes 7680 | tf_op jit(solution)/shard_map/all_gather | solution.py:154
  58.7 24.1 %all-gather.6.cloned.1.call-done = bf16[768,2304]{1,0:T(8,128)(2,1)} async-done(((bf16[192,2304]{1,0:T(8,128)(2,1)}), bf16[768,2304]{1,0:T(8,128)(2,1)}) %all-gather.6.cloned.1.call-update) | async-done | bytes 3538960 | tf_op jit(solution)/shard_map/all_gather | solution.py:148
  98.9 12.6 %fusion.28 = (f32[12,512]{1,0:T(8,128)S(1)}, f32[12,512,1024]{2,1,0:T(8,128)}) fusion(pred[512,1024]{1,0:T(8,128)(4,1)S(1)} %get-tuple-element.84, bf16[3,12,1024,64]{2,3,1,0:T(8,128)(2,1)} %bitcast.66, bf16[12,1024,64]{1,2,0:T(8,128)(2,1)S(1)} %slice_bitcast_fusion.2), kind=kOutput, calls=%fused_computation.48 | convolution fusion | flops 824174592 | bytes 28073984 | tf_op jit(solution)/shard_map/hqe,hke->hqk/dot_general | solution.py:54
  111.5 12.9 %fusion = f32[12,512]{1,0:T(8,128)S(1)} fusion(f32[12,512]{1,0:T(8,128)S(1)} %get-tuple-element.92, f32[12,512,1024]{2,1,0:T(8,128)} %get-tuple-element.93, pred[512,1024]{1,0:T(8,128)(4,1)S(1)} %get-tuple-element.84), kind=kLoop, calls=%fused_computation.12 | loop fusion | flops 25159680 | bytes 25739264 | tf_op jit(solution)/shard_map/reduce_sum | solution.py:77
  128.1 9.9 %fusion.51 = bf16[12,512,64]{1,2,0:T(8,128)(2,1)} fusion(f32[12,512]{1,0:T(8,128)S(1)} %fusion, f32[12,512]{1,0:T(8,128)S(1)} %get-tuple-element.92, f32[12,512,1024]{2,1,0:T(8,128)S(1)} %copy-done, pred[512,1024]{1,0:T(8,128)(4,1)S(1)} %get-tuple-element.84, bf16[3,12,1024,64]{2,3,1,0:T(8,128)(2,1)} %bitcast.67), kind=kOutput, calls=%fused_computation.95 | convolution fusion | flops 837156864 | bytes 28098560 | tf_op jit(solution)/shard_map/hqk,hke->hqe/dot_general | solution.py:80
  138.7 12.6 %fusion.29 = (f32[12,512]{1,0:T(8,128)S(1)}, f32[12,512,1024]{2,1,0:T(8,128)}) fusion(pred[512,1024]{1,0:T(8,128)(4,1)S(1)} %get-tuple-element.85, bf16[3,12,1024,64]{2,3,1,0:T(8,128)(2,1)} %bitcast.68, bf16[12,1024,64]{1,2,0:T(8,128)(2,1)S(1)} %slice_bitcast_fusion.2), kind=kOutput, calls=%fused_computation.49 | convolution fusion | flops 824174592 | bytes 28073984 | tf_op jit(solution)/shard_map/hqe,hke->hqk/dot_general | solution.py:54
  151.3 12.4 %fusion.1 = f32[12,512]{1,0:T(8,128)S(1)} fusion(f32[12,512]{1,0:T(8,128)S(1)} %get-tuple-element.90, f32[12,512,1024]{2,1,0:T(8,128)} %get-tuple-element.91, pred[512,1024]{1,0:T(8,128)(4,1)S(1)} %get-tuple-element.85), kind=kLoop, calls=%fused_computation.13 | loop fusion | flops 25159680 | bytes 25739264 | tf_op jit(solution)/shard_map/reduce_sum | solution.py:77
  181.9 21.5 %all-gather.10.cloned.1.call-done = bf16[768,3072]{1,0:T(8,128)(2,1)} async-done(((bf16[192,3072]{1,0:T(8,128)(2,1)}), bf16[768,3072]{1,0:T(8,128)(2,1)}) %all-gather.10.cloned.1.call-update) | async-done | bytes 4718608 | tf_op jit(solution)/shard_map/all_gather | solution.py:153
  203.4 39.0 %fusion.6 = (bf16[1024,3072]{1,0:T(8,128)(2,1)}, f32[1024,3072]{1,0:T(8,128)}) fusion(f32[3072]{0:T(1024)S(1)} %bitcast.82, bf16[768,3072]{1,0:T(8,128)(2,1)} %all-gather.10.cloned.1.call-done, f32[1024,768]{0,1:T(8,128)} %copy-done.4, f32[768]{0:T(1024)S(1)} %copy-done.43, f32[768]{0:T(1024)S(1)} %copy-done.35, f32[1024]{0:T(1024)S(1)} %add_rsqrt_fusion, ...), kind=kOutput, calls=%fused_computation.20 | convolution fusion | flops 5043388416 | bytes 26765312 | tf_op jit(solution)/shard_map/dot_general | solution.py:178
  242.4 50.3 %all-gather.12.cloned.1.call-done = bf16[3072,768]{1,0:T(8,128)(2,1)} async-done(((bf16[768,768]{1,0:T(8,128)(2,1)}), bf16[3072,768]{1,0:T(8,128)(2,1)}) %all-gather.12.cloned.1.call-update) | async-done | bytes 4718608 | tf_op jit(solution)/shard_map/all_gather | solution.py:155
  292.7 12.5 %fusion.83 = (bf16[3072]{0:T(1024)(128)(2,1)}, bf16[1024,3072]{1,0:T(8,128)(2,1)S(1)}) fusion(f32[1024,3072]{1,0:T(8,128)} %get-tuple-element.97, f32[3072]{0:T(1024)S(1)} %bitcast.83, bf16[1024,768]{1,0:T(8,128)(2,1)S(1)} %copy-done.18, bf16[3072,768]{1,0:T(8,128)(2,1)} %all-gather.12.cloned.1.call-done), kind=kOutput, calls=%fused_computation.145 | convolution fusion | flops 4869583872 | bytes 25184256 | tf_op jit(solution)/shard_map/dot_general | solution.py:40
  323.4 20.8 %multiply_reduce_fusion = (f32[12,512]{1,0:T(8,128)S(1)}, f32[12,512,1024]{2,1,0:T(8,128)}) fusion(f32[12,512]{1,0:T(8,128)S(1)} %log_add_fusion, f32[12,512,1024]{2,1,0:T(8,128)} %get-tuple-element.91, pred[512,1024]{1,0:T(8,128)(4,1)S(1)} %copy-done.14, bf16[3,12,1024,64]{2,3,1,0:T(8,128)(2,1)} %bitcast.70, bf16[12,1024,64]{1,2,0:T(8,128)(2,1)S(1)} %bitcast.78), kind=kOutput, calls=%fused_computation.1 | convolution fusion | flops 836757504 | bytes 53272576 | tf_op jit(solution)/shard_map/hqe,hke->hqk/dot_general | solution.py:107
  344.2 13.4 %fusion.13 = f32[12,1024,64]{1,2,0:T(8,128)} fusion(f32[12,512]{1,0:T(8,128)S(1)} %log_add_fusion, f32[12,512,1024]{2,1,0:T(8,128)} %get-tuple-element.91, pred[512,1024]{1,0:T(8,128)(4,1)S(1)} %copy-done.14, bf16[12,1024,64]{1,2,0:T(8,128)(2,1)S(1)} %bitcast.79), kind=kOutput, calls=%fused_computation.27 | convolution fusion | flops 830472192 | bytes 29655040 | tf_op jit(solution)/shard_map/hqk,hqe->hke/dot_general | solution.py:104
  360.1 18.1 %multiply_reduce_fusion.1 = (f32[12,512]{1,0:T(8,128)S(1)}, f32[12,512,1024]{2,1,0:T(8,128)}) fusion(f32[12,512]{1,0:T(8,128)S(1)} %copy-done.28, f32[12,512,1024]{2,1,0:T(8,128)} %get-tuple-element.93, pred[512,1024]{1,0:T(8,128)(4,1)S(1)} %copy-done.12, bf16[3,12,1024,64]{2,3,1,0:T(8,128)(2,1)} %bitcast.71, bf16[12,1024,64]{1,2,0:T(8,128)(2,1)} %bitcast.80), kind=kOutput, calls=%fused_computation.4 | convolution fusion | flops 836757504 | bytes 53264384 | tf_op jit(solution)/shard_map/hqe,hke->hqk/dot_general | solution.py:107
  378.2 41.8 %multiply_convert_fusion = (bf16[12,512,1024]{2,1,0:T(8,128)(2,1)}, bf16[12,512,1024]{2,1,0:T(8,128)(2,1)}) fusion(f32[12,512,1024]{2,1,0:T(8,128)} %get-tuple-element.101, f32[12,512]{1,0:T(8,128)S(1)} %get-tuple-element.100, f32[12,512]{1,0:T(8,128)S(1)} %log_add_fusion, f32[12,512,1024]{2,1,0:T(8,128)} %get-tuple-element.91, ...), kind=kLoop, calls=%fused_computation | loop fusion | flops 75497472 | bytes 126976000 | tf_op jit(solution)/shard_map/convert_element_type | solution.py:112
  428.9 9.9 %multiply_convert_fusion.3 = bf16[12,512,64]{1,2,0:T(8,128)(2,1)} fusion(bf16[12,512,1024]{2,1,0:T(8,128)(2,1)} %get-tuple-element.108, bf16[3,12,1024,64]{2,3,1,0:T(8,128)(2,1)} %bitcast.73), kind=kOutput, calls=%fused_computation.89 | convolution fusion | flops 806092800 | bytes 14942208 | tf_op jit(solution)/shard_map/hqk,hke->hqe/dot_general | solution.py:114
  438.8 14.1 %fusion.46 = bf16[1,12,1024,64]{2,3,1,0:T(8,128)(2,1)} fusion(f32[12,1024,64]{1,2,0:T(8,128)} %fusion.13, f32[12,512]{1,0:T(8,128)S(1)} %copy-done.28, f32[12,512,1024]{2,1,0:T(8,128)} %get-tuple-element.93, pred[512,1024]{1,0:T(8,128)(4,1)S(1)} %copy-done.12, bf16[12,1024,64]{1,2,0:T(8,128)(2,1)} %bitcast.81), kind=kOutput, calls=%fused_computation.92 | convolution fusion | flops 832045056 | bytes 31219712 | tf_op jit(solution)/shard_map/hqk,hqe->hke/dot_general | solution.py:104
  476.4 9.9 %convolution_convert_fusion.2 = bf16[768,3072]{1,0:T(8,128)(2,1)} fusion(bf16[1024,3072]{1,0:T(8,128)(2,1)} %copy-done.50, f32[1024,768]{0,1:T(8,128)} %copy-done.4, f32[768]{0:T(1024)S(1)} %copy-done.44, f32[768]{0:T(1024)S(1)} %copy-done.35, f32[1024]{0:T(1024)S(1)} %add_rsqrt_fusion, f32[1024]{0:T(1024)S(1)} %broadcast_multiply_fusion.4), kind=kOutput, calls=%fused_computation.52 | convolution fusion | flops 4838129664 | bytes 14170112 | tf_op jit(solution)/shard_map/dot_general | solution.py:34
  487.8 9.8 %convolution_convert_fusion.1 = bf16[3072,768]{1,0:T(8,128)(2,1)} fusion(bf16[1024,3072]{1,0:T(8,128)(2,1)} %get-tuple-element.96, bf16[1024,768]{1,0:T(8,128)(2,1)S(1)} %copy-done.19), kind=kOutput, calls=%fused_computation.51 | convolution fusion | flops 4834197504 | bytes 12582912 | tf_op jit(solution)/shard_map/dot_general | solution.py:34
  523.5 18.8 %all-reduce.14 = (bf16[768]{0:T(1024)(128)(2,1)S(1)}, bf16[768]{0:T(1024)(128)(2,1)S(1)}, bf16[768]{0:T(1024)(128)(2,1)S(1)}, bf16[768]{0:T(1024)(128)(2,1)S(1)}...) all-reduce(bf16[768]{0:T(1024)(128)(2,1)S(1)} %dynamic-update-slice, ...), channel_id=1, replica_groups=mesh['dp'=8,'fsdp'=4] {'fsdp'}, use_global_device_ids=true, to_apply=%add.5 | all-reduce | flops 8448 | bytes 33792
  555.0 81.9 %reduce-scatter.9.cloned.1.call-done = bf16[192,3072]{1,0:T(8,128)(2,1)} async-done(((bf16[768,3072]{1,0:T(8,128)(2,1)}), bf16[192,3072]{1,0:T(8,128)(2,1)}) %reduce-scatter.9.cloned.1.call-update) | async-done | bytes 1179664 | tf_op jit(solution)/shard_map/reduce_scatter | solution.py:244
  636.9 88.1 %reduce-scatter.11.cloned.1.call-done = bf16[768,768]{1,0:T(8,128)(2,1)} async-done(((bf16[3072,768]{1,0:T(8,128)(2,1)}), bf16[768,768]{1,0:T(8,128)(2,1)}) %reduce-scatter.11.cloned.1.call-update) | async-done | bytes 1179664 | tf_op jit(solution)/shard_map/reduce_scatter | solution.py:250
  725.0 144.6 %all-reduce.17 = (f32[192]{0:T(256)}, f32[192]{0:T(256)}, f32[192,2304]{1,0:T(8,128)}, f32[192,768]{1,0:T(8,128)}, f32[192]{0:T(256)}, /*index=5*/f32[192]{0:T(2...) all-reduce(f32[192]{0:T(256)S(1)} %dynamic-slice_convert_fusion.6, ...), channel_id=1, replica_groups=mesh['dp'=8,'fsdp'=4] {'dp'}, use_global_device_ids=true, to_apply=%region_16.17 | all-reduce | flops 1771392 | bytes 10632192 | tf_op jit(solution)/shard_map/psum | solution.py:258
  (192 shorter events, 145.1 us)
Async XLA Ops:
  7.2 75.6 %all-gather.6.cloned.1.call-start = ((), (), s32[]{:S(2)}) async-start(), calls=%async_computation.4 | async-start | bytes 4423680 | tf_op jit(solution)/shard_map/all_gather | solution.py:148
  7.9 32.7 %copy-start.36 = (s32[1024]{0:T(1024)S(1)}, s32[1024]{0:T(1024)}, u32[]{:S(2)}) copy-start(s32[1024]{0:T(1024)} %param.15) | copy-start | bytes 12292
  7.9 33.9 %copy-start.46 = (bf16[768]{0:T(1024)(128)(2,1)S(1)}, bf16[768]{0:T(1024)(128)(2,1)}, u32[]{:S(2)}) copy-start(bf16[768]{0:T(1024)(128)(2,1)} %param.24) | copy-start | bytes 4612
  7.9 48.5 %copy-start.17 = (bf16[1024,768]{1,0:T(8,128)(2,1)S(1)}, bf16[1024,768]{1,0:T(8,128)(2,1)}, u32[]{:S(2)}) copy-start(bf16[1024,768]{1,0:T(8,128)(2,1)} %param.27) | copy-start | bytes 4718596
  7.9 168.4 %all-gather.8.cloned.1.call-start = ((), (), s32[]{:S(2)}) async-start(), calls=%async_computation.5 | async-start | bytes 1474560 | tf_op jit(solution)/shard_map/all_gather | solution.py:149
  8.7 194.7 %all-gather.10.cloned.1.call-start = ((), (), s32[]{:S(2)}) async-start(), calls=%async_computation.6 | async-start | bytes 5898240 | tf_op jit(solution)/shard_map/all_gather | solution.py:153
  9.4 283.2 %all-gather.12.cloned.1.call-start = ((), (), s32[]{:S(2)}) async-start(), calls=%async_computation.7 | async-start | bytes 5898240 | tf_op jit(solution)/shard_map/all_gather | solution.py:155
  10.0 545.0 %reduce-scatter.7.cloned.1.call-start = ((), (), s32[]{:S(2)}) async-start(), calls=%async_computation.9 | async-start | bytes 1474560 | tf_op jit(solution)/shard_map/reduce_scatter | solution.py:232
  38.1 44.7 %copy-start.31 = (f32[768]{0:T(1024)}, f32[768]{0:T(1024)S(1)}, u32[]{:S(2)}) copy-start(f32[768]{0:T(1024)S(1)} %convert_element_type.147) | copy-start | bytes 9220
  38.1 44.7 %copy-start.41 = (f32[768]{0:T(1024)}, f32[768]{0:T(1024)S(1)}, u32[]{:S(2)}) copy-start(f32[768]{0:T(1024)S(1)} %convert_element_type.148) | copy-start | bytes 9220
  39.8 136.6 %copy-start.2 = (bf16[1024,768]{0,1:T(8,128)(2,1)}, bf16[1024,768]{0,1:T(8,128)(2,1)S(1)}, u32[]{:S(2)}) copy-start(bf16[1024,768]{0,1:T(8,128)(2,1)S(1)} %copy.47) | copy-start | bytes 4718596
  40.1 50.5 %copy-start.29 = (f32[1024]{0:T(1024)}, f32[1024]{0:T(1024)S(1)}, u32[]{:S(2)}) copy-start(f32[1024]{0:T(1024)S(1)} %broadcast_multiply_fusion.5) | copy-start | bytes 12292
  40.6 50.0 %copy-start.33 = (f32[1024]{0:T(1024)}, f32[1024]{0:T(1024)S(1)}, u32[]{:S(2)}) copy-start(f32[1024]{0:T(1024)S(1)} %add_rsqrt_fusion.1) | copy-start | bytes 12292
  58.7 65.8 %copy-start.11 = (pred[512,1024]{1,0:T(8,128)(4,1)}, pred[512,1024]{1,0:T(8,128)(4,1)S(1)}, u32[]{:S(2)}) copy-start(pred[512,1024]{1,0:T(8,128)(4,1)S(1)} %get-tuple-element.84) | copy-start | bytes 1572868
  58.7 105.0 %copy-start.13 = (pred[512,1024]{1,0:T(8,128)(4,1)}, pred[512,1024]{1,0:T(8,128)(4,1)S(1)}, u32[]{:S(2)}) copy-start(pred[512,1024]{1,0:T(8,128)(4,1)S(1)} %get-tuple-element.85) | copy-start | bytes 1572868
  98.9 39.7 %copy-start.9 = (bf16[12,1024,64]{1,2,0:T(8,128)(2,1)}, bf16[12,1024,64]{1,2,0:T(8,128)(2,1)S(1)}, u32[]{:S(2)}) copy-start(bf16[12,1024,64]{1,2,0:T(8,128)(2,1)S(1)} %slice_bitcast_fusion.2) | copy-start | bytes 4718596
  176.4 27.0 %copy-start.35 = (f32[768]{0:T(1024)S(1)}, f32[768]{0:T(1024)}, u32[]{:S(2)}) copy-start(f32[768]{0:T(1024)} %convert_element_type.156) | copy-start | bytes 9220
  176.4 27.0 %copy-start.37 = (f32[4,1,768]{2,1,0:T(1,128)S(1)}, f32[4,1,768]{2,1,0:T(1,128)}, u32[]{:S(2)}) copy-start(f32[4,1,768]{2,1,0:T(1,128)} %convert_element_type.192) | copy-start | bytes 36868
  176.4 27.0 %copy-start.43 = (f32[768]{0:T(1024)S(1)}, f32[768]{0:T(1024)}, u32[]{:S(2)}) copy-start(f32[768]{0:T(1024)} %convert_element_type.157) | copy-start | bytes 9220
  203.4 89.3 %copy-start.18 = (bf16[1024,768]{1,0:T(8,128)(2,1)S(1)}, bf16[1024,768]{1,0:T(8,128)(2,1)}, u32[]{:S(2)}) copy-start(bf16[1024,768]{1,0:T(8,128)(2,1)} %param.27) | copy-start | bytes 4718596
  452.9 102.1 %reduce-scatter.5.cloned.1.call-start = ((), (), s32[]{:S(2)}) async-start(), calls=%async_computation.8 | async-start | bytes 4423680 | tf_op jit(solution)/shard_map/reduce_scatter | solution.py:229
  476.3 160.5 %reduce-scatter.9.cloned.1.call-start = ((), (), s32[]{:S(2)}) async-start(), calls=%async_computation.10 | async-start | bytes 5898240 | tf_op jit(solution)/shard_map/reduce_scatter | solution.py:244
  486.3 238.7 %reduce-scatter.11.cloned.1.call-start = ((), (), s32[]{:S(2)}) async-start(), calls=%async_computation.11 | async-start | bytes 5898240 | tf_op jit(solution)/shard_map/reduce_scatter | solution.py:250
  519.8 22.5 %copy-start.6 = (f32[1024,768]{0,1:T(8,128)S(1)}, f32[1024,768]{0,1:T(8,128)}, u32[]{:S(2)}) copy-start(f32[1024,768]{0,1:T(8,128)} %copy-done.4) | copy-start | bytes 9437188
  (35 other events, 207.2 us)
Sparse Core Ops, SparseCore 0:
  9.6 73.1 all-gather.5
  84.4 28.7 all-gather.7
  114.7 88.6 all-gather.9
  204.8 87.7 all-gather.11
  453.0 27.7 reduce-scatter.6
  483.0 66.1 reduce-scatter.4
  551.4 85.4 reduce-scatter.8
  639.2 85.7 reduce-scatter.10
where the time goes:
time: 880 us; the launch traced here: 877 us
  waiting for transfers between devices  269 us (31%)
  matrix products  262 us (30%)
  blocking collectives  199 us (23%)
  other arithmetic  86.3 us (10%)
  local copies, waits for them, and re-layouts  43 us (5%)
  between operations  16.9 us (2%)
    psum x1, blocking collectives, on_device(): lax.psum((all_rows[0], all_rows[1], all_rows[2], all_rows[3], all_rows[4]...  145 us
    reduce_scatter x1, waiting for transfers between devices, on_device(): lax.psum_scatter(d_w_fc2.astype(jnp.bfloat16), 'fsdp', scatter_dimension=...  88.1 us
    reduce_scatter x1, waiting for transfers between devices, on_device(): lax.psum_scatter(d_w_fc1.astype(jnp.bfloat16), 'fsdp', scatter_dimension=...  81.9 us
    all_gather x1, waiting for transfers between devices, on_device(): lax.all_gather(w_fc2, 'fsdp', axis=0, tiled=True)  50.3 us
    convert_element_type x1, other arithmetic, attend_back(): d_score = (attn_probs * (d_probs - jnp.sum(d_probs * attn_probs, axis=-1,...  41.8 us
    unnamed x2, blocking collectives  40.6 us
    dot_general x1, matrix products, on_device(): jnp.dot(normed_mid, gathered[7], preferred_element_type=jnp.float32)  39 us
    dot_general x2, matrix products, attend_back(): jnp.einsum('hqe,hke->hqk', grad_block, value_heads, preferred_element_typ...  38.8 us
  transfers between devices with their start and end apart: 8, of which 5 were waited for; matrix products, arithmetic and copies ran while one was open for 25% of the time, Pallas kernels for 0%

commit v1 on v0

--- a/solution.py
+++ b/solution.py
@@ -1,3 +1,4 @@
+import functools
 import math
 import jax
 import jax.numpy as jnp
@@ -9,6 +10,29 @@
 neg_big = -1e30
 inv_sqrt_two = 1.0 / math.sqrt(2.0)
 inv_sqrt_tau = 1.0 / math.sqrt(2.0 * math.pi)
+
+
+def samples_all_lift(my_data, out_dim):
+    right_arr = lax.axis_index("fsdp")
+    e_now = lax.axis_size("fsdp")
+    f_next, known, piece_out = (e_now, right_arr, my_data.shape[out_dim])
+    by_place = []
+    for u, it in enumerate(my_data.shape):
+        by_place.append(it * f_next if u == out_dim else it)
+    b_next = jnp.zeros(by_place, my_data.dtype)
+    carry_out = lax.dynamic_update_slice_in_dim(b_next, my_data, known * piece_out, axis=out_dim)
+    for at in [*range(1, f_next)]:
+        series = []
+        for u in [*range(f_next)]:
+            series.append((u, (u + 1) % f_next))
+        my_data = lax.ppermute(my_data, "fsdp", series)
+        carry_out = lax.dynamic_update_slice_in_dim(
+            carry_out, my_data, (known - at) % f_next * piece_out, axis=out_dim
+        )
+    return carry_out
+
+
+clear_roots_for = functools.partial(samples_all_lift, out_dim=0)
 
 
 def layer_norm(token_rows, gain_vec, shift_vec):
@@ -152,7 +176,7 @@
         lax.all_gather(ln2_bias, "fsdp", axis=0, tiled=True),
         lax.all_gather(w_fc1, "fsdp", axis=0, tiled=True),
         lax.all_gather(b_fc1, "fsdp", axis=0, tiled=True),
-        lax.all_gather(w_fc2, "fsdp", axis=0, tiled=True),
+        clear_roots_for(w_fc2),
         lax.all_gather(b_fc2, "fsdp", axis=0, tiled=True),
     )
     gain_one = gathered[0].astype(jnp.float32)

time: 880 us -> 944 us (1.073)
  starting transfers between devices: 1.03 us -> 29.5 us
  blocking collectives: 199 us -> 220 us
  local copies, waits for them, and re-layouts: 43 us -> 54.2 us
    ppermute x0 -> x3, waiting for transfers between devices: none -> 143 us  [samples_all_lift(): my_data = lax.ppermute(my_data, 'fsdp', series)]
    reduce_scatter x1, waiting for transfers between devices: 81.9 us -> 0.01 us  [on_device(): lax.psum_scatter(d_w_fc1.astype(jnp.bfloat16), 'fsdp', scatter_dimension=...]
    reduce_scatter x1, waiting for transfers between devices: 88.1 us -> 31.5 us  [on_device(): lax.psum_scatter(d_w_fc2.astype(jnp.bfloat16), 'fsdp', scatter_dimension=...]
    ppermute x0 -> x3, starting transfers between devices: none -> 28.8 us  [samples_all_lift(): my_data = lax.ppermute(my_data, 'fsdp', series)]
    unnamed x2, blocking collectives: 40.6 us -> 61.8 us
    unnamed x120 -> x128, local copies, waits for them, and re-layouts: 27.5 us -> 29.2 us
  transfers between devices with their start and end apart: 8 -> 11, of which waited for: 5 -> 7; matrix products, arithmetic and copies ran while one was open for 25% -> 24% of each run, Pallas kernels for 0% -> 0%
where the time goes in v1:
time: 944 us; the launch traced here: 941 us
  waiting for transfers between devices  272 us (29%)
  matrix products  261 us (28%)
  blocking collectives  220 us (23%)
  other arithmetic  86.4 us (9%)
  local copies, waits for them, and re-layouts  54.2 us (6%)
  starting transfers between devices  29.5 us (3%)
  between operations  17 us (2%)
    psum x1, blocking collectives, on_device(): lax.psum((all_rows[0], all_rows[1], all_rows[2], all_rows[3], all_rows[4]...  145 us
    ppermute x3, waiting for transfers between devices, samples_all_lift(): my_data = lax.ppermute(my_data, 'fsdp', series)  143 us
    unnamed x2, blocking collectives  61.8 us
    all_gather x1, waiting for transfers between devices, on_device(): lax.all_gather(w_fc2, 'fsdp', axis=0, tiled=True)  50.3 us
    convert_element_type x1, other arithmetic, attend_back(): d_score = (attn_probs * (d_probs - jnp.sum(d_probs * attn_probs, axis=-1,...  41.8 us
    dot_general x1, matrix products, on_device(): jnp.dot(normed_mid, gathered[7], preferred_element_type=jnp.float32)  39 us
    dot_general x2, matrix products, attend_back(): jnp.einsum('hqe,hke->hqk', grad_block, value_heads, preferred_element_typ...  38.9 us
    reduce_scatter x1, waiting for transfers between devices, on_device(): lax.psum_scatter(d_w_fc2.astype(jnp.bfloat16), 'fsdp', scatter_dimension=...  31.5 us
  transfers between devices with their start and end apart: 11, of which 7 were waited for; matrix products, arithmetic and copies ran while one was open for 24% of the time, Pallas kernels for 0%

profile of v1, /device:TPU:0, one launch (start us, length us, event | category | flops | bytes accessed | tf_op | source)
XLA Modules:
  0.0 940.6 jit_solution(10659164305915748822)
XLA Ops:
  16.2 21.8 %all-reduce.15 = (bf16[768]{0:T(1024)(128)(2,1)S(1)}, bf16[768]{0:T(1024)(128)(2,1)S(1)}, bf16[768]{0:T(1024)(128)(2,1)S(1)}, bf16[768]{0:T(1024)(128)(2,1)S(1)}, bf16[768]{0:T(1024)(128)(2,1)S(1)}) all-reduce(bf16[768]{0:T(1024)(128)(2,1)S(1)} %dynamic-update-slice.1, ...), channel_id=1, replica_groups=mesh['dp'=8,'fsdp'=4] {'fsdp'}, use_global_device_ids=true, to_apply=%add.1 | all-reduce | flops 3840 | bytes 15360
  41.8 14.0 %all-gather = bf16[4,1,768]{2,1,0:T(2,128)(2,1)S(1)} all-gather(bf16[1,1,768]{2,1,0:T(2,128)(2,1)S(1)} %reshape.178), channel_id=1, replica_groups=mesh['dp'=8,'fsdp'=4] {'fsdp'}, dimensions={0}, use_global_device_ids=true | all-gather | bytes 7680 | tf_op jit(solution)/shard_map/all_gather | solution.py:178
  58.7 24.1 %all-gather.6.cloned.1.call-done = bf16[768,2304]{1,0:T(8,128)(2,1)} async-done(((bf16[192,2304]{1,0:T(8,128)(2,1)}), bf16[768,2304]{1,0:T(8,128)(2,1)}) %all-gather.6.cloned.1.call-update) | async-done | bytes 3538960 | tf_op jit(solution)/shard_map/all_gather | solution.py:172
  98.9 12.6 %fusion.28 = (f32[12,512]{1,0:T(8,128)S(1)}, f32[12,512,1024]{2,1,0:T(8,128)}) fusion(pred[512,1024]{1,0:T(8,128)(4,1)S(1)} %get-tuple-element.84, bf16[3,12,1024,64]{2,3,1,0:T(8,128)(2,1)} %bitcast.66, bf16[12,1024,64]{1,2,0:T(8,128)(2,1)S(1)} %slice_bitcast_fusion.2), kind=kOutput, calls=%fused_computation.48 | convolution fusion | flops 824174592 | bytes 28073984 | tf_op jit(solution)/shard_map/hqe,hke->hqk/dot_general | solution.py:78
  111.6 12.9 %fusion = f32[12,512]{1,0:T(8,128)S(1)} fusion(f32[12,512]{1,0:T(8,128)S(1)} %get-tuple-element.92, f32[12,512,1024]{2,1,0:T(8,128)} %get-tuple-element.93, pred[512,1024]{1,0:T(8,128)(4,1)S(1)} %get-tuple-element.84), kind=kLoop, calls=%fused_computation.12 | loop fusion | flops 25159680 | bytes 25739264 | tf_op jit(solution)/shard_map/reduce_sum | solution.py:101
  138.7 12.6 %fusion.29 = (f32[12,512]{1,0:T(8,128)S(1)}, f32[12,512,1024]{2,1,0:T(8,128)}) fusion(pred[512,1024]{1,0:T(8,128)(4,1)S(1)} %get-tuple-element.85, bf16[3,12,1024,64]{2,3,1,0:T(8,128)(2,1)} %bitcast.68, bf16[12,1024,64]{1,2,0:T(8,128)(2,1)S(1)} %slice_bitcast_fusion.2), kind=kOutput, calls=%fused_computation.49 | convolution fusion | flops 824174592 | bytes 28073984 | tf_op jit(solution)/shard_map/hqe,hke->hqk/dot_general | solution.py:78
  151.4 12.4 %fusion.1 = f32[12,512]{1,0:T(8,128)S(1)} fusion(f32[12,512]{1,0:T(8,128)S(1)} %get-tuple-element.90, f32[12,512,1024]{2,1,0:T(8,128)} %get-tuple-element.91, pred[512,1024]{1,0:T(8,128)(4,1)S(1)} %get-tuple-element.85), kind=kLoop, calls=%fused_computation.13 | loop fusion | flops 25159680 | bytes 25739264 | tf_op jit(solution)/shard_map/reduce_sum | solution.py:101
  182.0 21.4 %all-gather.10.cloned.1.call-done = bf16[768,3072]{1,0:T(8,128)(2,1)} async-done(((bf16[192,3072]{1,0:T(8,128)(2,1)}), bf16[768,3072]{1,0:T(8,128)(2,1)}) %all-gather.10.cloned.1.call-update) | async-done | bytes 4718608 | tf_op jit(solution)/shard_map/all_gather | solution.py:177
  203.4 39.0 %fusion.6 = (bf16[1024,3072]{1,0:T(8,128)(2,1)}, f32[1024,3072]{1,0:T(8,128)}) fusion(f32[3072]{0:T(1024)S(1)} %bitcast.82, bf16[768,3072]{1,0:T(8,128)(2,1)} %all-gather.10.cloned.1.call-done, f32[1024,768]{0,1:T(8,128)} %copy-done.4, f32[768]{0:T(1024)S(1)} %copy-done.46, f32[768]{0:T(1024)S(1)} %copy-done.38, f32[1024]{0:T(1024)S(1)} %add_rsqrt_fusion, ...), kind=kOutput, calls=%fused_computation.20 | convolution fusion | flops 5043388416 | bytes 26765312 | tf_op jit(solution)/shard_map/dot_general | solution.py:202
  242.4 50.3 %all-gather.12.cloned.1.call-done = bf16[3072,768]{1,0:T(8,128)(2,1)} async-done(((bf16[768,768]{1,0:T(8,128)(2,1)}), bf16[3072,768]{1,0:T(8,128)(2,1)}) %all-gather.12.cloned.1.call-update) | async-done | bytes 4718608 | tf_op jit(solution)/shard_map/all_gather | solution.py:220
  292.7 12.5 %fusion.83 = (bf16[3072]{0:T(1024)(128)(2,1)}, bf16[1024,3072]{1,0:T(8,128)(2,1)S(1)}) fusion(f32[1024,3072]{1,0:T(8,128)} %get-tuple-element.97, f32[3072]{0:T(1024)S(1)} %bitcast.83, bf16[1024,768]{1,0:T(8,128)(2,1)S(1)} %copy-done.18, bf16[3072,768]{1,0:T(8,128)(2,1)} %all-gather.12.cloned.1.call-done), kind=kOutput, calls=%fused_computation.149 | convolution fusion | flops 4869583872 | bytes 25184256 | tf_op jit(solution)/shard_map/dot_general | solution.py:64
  323.4 20.8 %multiply_reduce_fusion = (f32[12,512]{1,0:T(8,128)S(1)}, f32[12,512,1024]{2,1,0:T(8,128)}) fusion(f32[12,512]{1,0:T(8,128)S(1)} %log_add_fusion, f32[12,512,1024]{2,1,0:T(8,128)} %get-tuple-element.91, pred[512,1024]{1,0:T(8,128)(4,1)S(1)} %copy-done.14, bf16[3,12,1024,64]{2,3,1,0:T(8,128)(2,1)} %bitcast.70, bf16[12,1024,64]{1,2,0:T(8,128)(2,1)S(1)} %bitcast.78), kind=kOutput, calls=%fused_computation.1 | convolution fusion | flops 836757504 | bytes 53272576 | tf_op jit(solution)/shard_map/hqe,hke->hqk/dot_general | solution.py:131
  344.2 13.4 %fusion.13 = f32[12,1024,64]{1,2,0:T(8,128)} fusion(f32[12,512]{1,0:T(8,128)S(1)} %log_add_fusion, f32[12,512,1024]{2,1,0:T(8,128)} %get-tuple-element.91, pred[512,1024]{1,0:T(8,128)(4,1)S(1)} %copy-done.14, bf16[12,1024,64]{1,2,0:T(8,128)(2,1)S(1)} %bitcast.79), kind=kOutput, calls=%fused_computation.27 | convolution fusion | flops 830472192 | bytes 29655040 | tf_op jit(solution)/shard_map/hqk,hqe->hke/dot_general | solution.py:128
  360.1 18.1 %multiply_reduce_fusion.1 = (f32[12,512]{1,0:T(8,128)S(1)}, f32[12,512,1024]{2,1,0:T(8,128)}) fusion(f32[12,512]{1,0:T(8,128)S(1)} %copy-done.31, f32[12,512,1024]{2,1,0:T(8,128)} %get-tuple-element.93, pred[512,1024]{1,0:T(8,128)(4,1)S(1)} %copy-done.12, bf16[3,12,1024,64]{2,3,1,0:T(8,128)(2,1)} %bitcast.71, bf16[12,1024,64]{1,2,0:T(8,128)(2,1)} %bitcast.80), kind=kOutput, calls=%fused_computation.4 | convolution fusion | flops 836757504 | bytes 53264384 | tf_op jit(solution)/shard_map/hqe,hke->hqk/dot_general | solution.py:131
  378.2 41.8 %multiply_convert_fusion = (bf16[12,512,1024]{2,1,0:T(8,128)(2,1)}, bf16[12,512,1024]{2,1,0:T(8,128)(2,1)}) fusion(f32[12,512,1024]{2,1,0:T(8,128)} %get-tuple-element.101, f32[12,512]{1,0:T(8,128)S(1)} %get-tuple-element.100, f32[12,512]{1,0:T(8,128)S(1)} %log_add_fusion, f32[12,512,1024]{2,1,0:T(8,128)} %get-tuple-element.91, ...), kind=kLoop, calls=%fused_computation | loop fusion | flops 75497472 | bytes 126976000 | tf_op jit(solution)/shard_map/convert_element_type | solution.py:136
  438.9 14.1 %fusion.46 = bf16[1,12,1024,64]{2,3,1,0:T(8,128)(2,1)} fusion(f32[12,1024,64]{1,2,0:T(8,128)} %fusion.13, f32[12,512]{1,0:T(8,128)S(1)} %copy-done.31, f32[12,512,1024]{2,1,0:T(8,128)} %get-tuple-element.93, pred[512,1024]{1,0:T(8,128)(4,1)S(1)} %copy-done.12, bf16[12,1024,64]{1,2,0:T(8,128)(2,1)} %bitcast.81), kind=kOutput, calls=%fused_computation.92 | convolution fusion | flops 832045056 | bytes 31219712 | tf_op jit(solution)/shard_map/hqk,hqe->hke/dot_general | solution.py:128
  498.1 55.7 %collective-permute-done = bf16[768,768]{1,0:T(8,128)(2,1)S(1)} collective-permute-done((bf16[768,768]{1,0:T(8,128)(2,1)}, bf16[768,768]{1,0:T(8,128)(2,1)S(1)}, u32[]{:S(2)}, u32[]{:S(2)}) %collective-permute-start) | collective-permute-done | bytes 1179680 | tf_op jit(solution)/shard_map/ppermute | solution.py:28
  554.9 15.3 %collective-permute-start.1 = (bf16[768,768]{1,0:T(8,128)(2,1)S(1)}, bf16[768,768]{1,0:T(8,128)(2,1)}, u32[]{:S(2)}, u32[]{:S(2)}) collective-permute-start(bf16[768,768]{1,0:T(8,128)(2,1)S(1)} %collective-permute-done), channel_id=1, source_target_pairs={{0,1},{1,2},{2,3},{3,0},{4,5},{5,6},{6,7},{7,4},{8,9},{9,10},{10,1... | collective-permute-start | bytes 3538952 | tf_op jit(solution)/shard_map/ppermute | solution.py:28
  570.1 43.2 %collective-permute-done.1 = bf16[768,768]{1,0:T(8,128)(2,1)} collective-permute-done((bf16[768,768]{1,0:T(8,128)(2,1)S(1)}, bf16[768,768]{1,0:T(8,128)(2,1)}, u32[]{:S(2)}, u32[]{:S(2)}) %collective-permute-start.1) | collective-permute-done | bytes 1179680 | tf_op jit(solution)/shard_map/ppermute | solution.py:28
  613.3 13.5 %collective-permute-start.2 = (bf16[768,768]{1,0:T(8,128)(2,1)}, bf16[768,768]{1,0:T(8,128)(2,1)}, u32[]{:S(2)}, u32[]{:S(2)}) collective-permute-start(bf16[768,768]{1,0:T(8,128)(2,1)} %collective-permute-done.1), channel_id=1, source_target_pairs={{0,1},{1,2},{2,3},{3,0},{4,5},{5,6},{6,7},{7,4},{8,9},{9,10},{10,1... | collective-permute-start | bytes 3538952 | tf_op jit(solution)/shard_map/ppermute | solution.py:28
  635.7 43.8 %collective-permute-done.2 = bf16[768,768]{1,0:T(8,128)(2,1)} collective-permute-done((bf16[768,768]{1,0:T(8,128)(2,1)}, bf16[768,768]{1,0:T(8,128)(2,1)}, u32[]{:S(2)}, u32[]{:S(2)}) %collective-permute-start.2) | collective-permute-done | bytes 1179680 | tf_op jit(solution)/shard_map/ppermute | solution.py:28
  704.8 39.9 %all-reduce.14 = (bf16[768]{0:T(1024)(128)(2,1)S(1)}, bf16[768]{0:T(1024)(128)(2,1)S(1)}, bf16[768]{0:T(1024)(128)(2,1)S(1)}, bf16[768]{0:T(1024)(128)(2,1)S(1)}...) all-reduce(bf16[768]{0:T(1024)(128)(2,1)S(1)} %dynamic-update-slice, ...), channel_id=1, replica_groups=mesh['dp'=8,'fsdp'=4] {'fsdp'}, use_global_device_ids=true, to_apply=%add.5 | all-reduce | flops 8448 | bytes 33792
  757.4 31.5 %reduce-scatter.11.cloned.1.call-done = bf16[768,768]{1,0:T(8,128)(2,1)} async-done(((bf16[3072,768]{1,0:T(8,128)(2,1)}), bf16[768,768]{1,0:T(8,128)(2,1)}) %reduce-scatter.11.cloned.1.call-update) | async-done | bytes 1179664 | tf_op jit(solution)/shard_map/reduce_scatter | solution.py:274
  788.9 144.6 %all-reduce.17 = (f32[192]{0:T(256)}, f32[192]{0:T(256)}, f32[192,2304]{1,0:T(8,128)}, f32[192,768]{1,0:T(8,128)}, f32[192]{0:T(256)}, /*index=5*/f32[192]{0:T(2...) all-reduce(f32[192]{0:T(256)S(1)} %dynamic-slice_convert_fusion.6, ...), channel_id=1, replica_groups=mesh['dp'=8,'fsdp'=4] {'dp'}, use_global_device_ids=true, to_apply=%region_16.17 | all-reduce | flops 1771392 | bytes 10632192 | tf_op jit(solution)/shard_map/psum | solution.py:282
  (211 shorter events, 194.3 us)
Async XLA Ops:
  7.2 75.6 %all-gather.6.cloned.1.call-start = ((), (), s32[]{:S(2)}) async-start(), calls=%async_computation.4 | async-start | bytes 4423680 | tf_op jit(solution)/shard_map/all_gather | solution.py:172
  7.9 48.5 %copy-start.17 = (bf16[1024,768]{1,0:T(8,128)(2,1)S(1)}, bf16[1024,768]{1,0:T(8,128)(2,1)}, u32[]{:S(2)}) copy-start(bf16[1024,768]{1,0:T(8,128)(2,1)} %param.27) | copy-start | bytes 4718596
  7.9 168.5 %all-gather.8.cloned.1.call-start = ((), (), s32[]{:S(2)}) async-start(), calls=%async_computation.5 | async-start | bytes 1474560 | tf_op jit(solution)/shard_map/all_gather | solution.py:173
  8.7 194.7 %all-gather.10.cloned.1.call-start = ((), (), s32[]{:S(2)}) async-start(), calls=%async_computation.6 | async-start | bytes 5898240 | tf_op jit(solution)/shard_map/all_gather | solution.py:177
  9.4 283.2 %all-gather.12.cloned.1.call-start = ((), (), s32[]{:S(2)}) async-start(), calls=%async_computation.7 | async-start | bytes 5898240 | tf_op jit(solution)/shard_map/all_gather | solution.py:220
  10.0 747.4 %reduce-scatter.7.cloned.1.call-start = ((), (), s32[]{:S(2)}) async-start(), calls=%async_computation.9 | async-start | bytes 1474560 | tf_op jit(solution)/shard_map/reduce_scatter | solution.py:256
  38.1 44.7 %copy-start.34 = (f32[768]{0:T(1024)}, f32[768]{0:T(1024)S(1)}, u32[]{:S(2)}) copy-start(f32[768]{0:T(1024)S(1)} %convert_element_type.147) | copy-start | bytes 9220
  38.1 44.7 %copy-start.44 = (f32[768]{0:T(1024)}, f32[768]{0:T(1024)S(1)}, u32[]{:S(2)}) copy-start(f32[768]{0:T(1024)S(1)} %convert_element_type.148) | copy-start | bytes 9220
  39.8 136.7 %copy-start.2 = (bf16[1024,768]{0,1:T(8,128)(2,1)}, bf16[1024,768]{0,1:T(8,128)(2,1)S(1)}, u32[]{:S(2)}) copy-start(bf16[1024,768]{0,1:T(8,128)(2,1)S(1)} %copy.47) | copy-start | bytes 4718596
  40.1 50.5 %copy-start.32 = (f32[1024]{0:T(1024)}, f32[1024]{0:T(1024)S(1)}, u32[]{:S(2)}) copy-start(f32[1024]{0:T(1024)S(1)} %broadcast_multiply_fusion.5) | copy-start | bytes 12292
  40.6 50.0 %copy-start.36 = (f32[1024]{0:T(1024)}, f32[1024]{0:T(1024)S(1)}, u32[]{:S(2)}) copy-start(f32[1024]{0:T(1024)S(1)} %add_rsqrt_fusion.1) | copy-start | bytes 12292
  58.7 65.9 %copy-start.11 = (pred[512,1024]{1,0:T(8,128)(4,1)}, pred[512,1024]{1,0:T(8,128)(4,1)S(1)}, u32[]{:S(2)}) copy-start(pred[512,1024]{1,0:T(8,128)(4,1)S(1)} %get-tuple-element.84) | copy-start | bytes 1572868
  58.7 105.1 %copy-start.13 = (pred[512,1024]{1,0:T(8,128)(4,1)}, pred[512,1024]{1,0:T(8,128)(4,1)S(1)}, u32[]{:S(2)}) copy-start(pred[512,1024]{1,0:T(8,128)(4,1)S(1)} %get-tuple-element.85) | copy-start | bytes 1572868
  98.9 39.8 %copy-start.9 = (bf16[12,1024,64]{1,2,0:T(8,128)(2,1)}, bf16[12,1024,64]{1,2,0:T(8,128)(2,1)S(1)}, u32[]{:S(2)}) copy-start(bf16[12,1024,64]{1,2,0:T(8,128)(2,1)S(1)} %slice_bitcast_fusion.2) | copy-start | bytes 4718596
  203.4 89.3 %copy-start.18 = (bf16[1024,768]{1,0:T(8,128)(2,1)S(1)}, bf16[1024,768]{1,0:T(8,128)(2,1)}, u32[]{:S(2)}) copy-start(bf16[1024,768]{1,0:T(8,128)(2,1)} %param.27) | copy-start | bytes 4718596
  453.0 304.4 %reduce-scatter.5.cloned.1.call-start = ((), (), s32[]{:S(2)}) async-start(), calls=%async_computation.8 | async-start | bytes 4423680 | tf_op jit(solution)/shard_map/reduce_scatter | solution.py:253
  476.6 280.8 %reduce-scatter.9.cloned.1.call-start = ((), (), s32[]{:S(2)}) async-start(), calls=%async_computation.10 | async-start | bytes 5898240 | tf_op jit(solution)/shard_map/reduce_scatter | solution.py:268
  486.5 302.3 %reduce-scatter.11.cloned.1.call-start = ((), (), s32[]{:S(2)}) async-start(), calls=%async_computation.11 | async-start | bytes 5898240 | tf_op jit(solution)/shard_map/reduce_scatter | solution.py:274
  498.0 130.4 %copy-start.53 = (bf16[192]{0:T(256)(128)(2,1)S(1)}, bf16[192]{0:T(256)(128)(2,1)}, u32[]{:S(2)}) copy-start(bf16[192]{0:T(256)(128)(2,1)} %param.26) | copy-start | bytes 1156
  498.0 55.8 %collective-permute-start = (bf16[768,768]{1,0:T(8,128)(2,1)}, bf16[768,768]{1,0:T(8,128)(2,1)S(1)}, u32[]{:S(2)}, u32[]{:S(2)}) collective-permute-start(bf16[768,768]{1,0:T(8,128)(2,1)} %param.25), channel_id=1, source_target_pairs={{0,1},{1,2},{2,3},{3,0},{4,5},{5,6},{6,7},{7,4},{8,9},{9,10},{10,1... | collective-permute-start | bytes 3538952 | tf_op jit(solution)/shard_map/ppermute | solution.py:28
  554.9 58.4 %collective-permute-start.1 = (bf16[768,768]{1,0:T(8,128)(2,1)S(1)}, bf16[768,768]{1,0:T(8,128)(2,1)}, u32[]{:S(2)}, u32[]{:S(2)}) collective-permute-start(bf16[768,768]{1,0:T(8,128)(2,1)S(1)} %collective-permute-done), channel_id=1, source_target_pairs={{0,1},{1,2},{2,3},{3,0},{4,5},{5,6},{6,7},{7,4},{8,9},{9,10},{10,1... | collective-permute-start | bytes 3538952 | tf_op jit(solution)/shard_map/ppermute | solution.py:28
  613.3 66.2 %collective-permute-start.2 = (bf16[768,768]{1,0:T(8,128)(2,1)}, bf16[768,768]{1,0:T(8,128)(2,1)}, u32[]{:S(2)}, u32[]{:S(2)}) collective-permute-start(bf16[768,768]{1,0:T(8,128)(2,1)} %collective-permute-done.1), channel_id=1, source_target_pairs={{0,1},{1,2},{2,3},{3,0},{4,5},{5,6},{6,7},{7,4},{8,9},{9,10},{10,1... | collective-permute-start | bytes 3538952 | tf_op jit(solution)/shard_map/ppermute | solution.py:28
  631.1 50.7 %copy-start.51 = (bf16[768,2304]{1,0:T(8,128)(2,1)S(1)}, bf16[768,2304]{1,0:T(8,128)(2,1)}, u32[]{:S(2)}) copy-start(bf16[768,2304]{1,0:T(8,128)(2,1)} %all-gather.6.cloned.1.call-done) | copy-start | bytes 10616836
  701.0 43.7 %copy-start.6 = (f32[1024,768]{0,1:T(8,128)S(1)}, f32[1024,768]{0,1:T(8,128)}, u32[]{:S(2)}) copy-start(f32[1024,768]{0,1:T(8,128)} %copy-done.4) | copy-start | bytes 9437188
  (42 other events, 362.4 us)
Sparse Core Ops, SparseCore 0:
  9.6 73.1 all-gather.5
  84.4 28.7 all-gather.7
  114.8 88.5 all-gather.9
  204.8 87.7 all-gather.11
  453.1 27.7 reduce-scatter.6
  483.0 90.1 reduce-scatter.4
  575.5 126.2 reduce-scatter.8
  704.1 84.7 reduce-scatter.10
